TPU v7x, 32 devices: a whole 2x2x4 slice. The times are simulated.
32 devices in a mesh: groups: 2 (over y), ctx: 4 (over z), head: 2 (over x), rep: 2 (over core).
Axes of the slice: x: 2, y: 2, z: 4, core: 2. Of those that a mesh axis runs over, the one named last changes fastest.
Arguments:
- queries: bfloat16 [1024, 5120], P(('groups', 'ctx'), 'head'), parts along dimension 0, may hold values from -50 to 50
- key_vectors: bfloat16 [1024, 5120], P(('groups', 'ctx'), 'head'), parts along dimension 0, may hold values from -5 to 5
- values: bfloat16 [1024, 5120], P(('groups', 'ctx'), 'head'), parts along dimension 0, may hold values from -6 to 6
- learn_rates: float32 [8, 1024], P('head', ('groups', 'ctx')), parts along dimension 1, may hold values from 0.02 to 0.2
- fast_weights: float32 [16, 3, 640, 640], P(('groups', 'head'), None, ('ctx', 'rep')), parts along dimension 0, may hold values from -0.25 to 0.25
- momentum: float32 [16, 3, 640, 640], P(('groups', 'head'), None, ('ctx', 'rep')), parts along dimension 0, may hold values from -0.25 to 0.25
Outputs:
- layer_output: bfloat16 [1024, 5120], P(('groups', 'ctx'), ('head', 'rep')), parts along dimension 0
- fast_updated: float32 [16, 3, 640, 640], P(('groups', 'head'), None, ('ctx', 'rep')), parts along dimension 0
There are 2 independent parts, one for each index of `groups`. A program takes and returns all parts, laid end to end along the dimension named above; each array names one. Nothing has to cross between parts.
All inputs are finite; a program needn't handle non-finite values.
Results may differ from a plain program's by a relative error of at most 0.038.
Values may be sent and summed in bfloat16 or wider, within the bound.
No kernel may reach another device: no remote copies, remote signals or barrier semaphores. Data moves between devices by JAX's collectives and lax.ppermute only.
A program may use at most 64 MiB of HBM per device.

v0:
```python
import jax
import jax.numpy as jnp
from jax import lax
from jax.sharding import PartitionSpec as P

epsilon = 1e-06
momentum_decay = 0.9


def passed_along(value, axis, steps):
    count = lax.axis_size(axis)
    initial, last = (max(0, -steps), min(count, count - steps))
    return lax.ppermute(value, axis, [(source, source + steps) for source in range(initial, last)])


def unit_rows(tensor):
    widened = tensor.astype(jnp.float32)
    factor = lax.rsqrt(jnp.mean(widened * widened, axis=-1, keepdims=True) + epsilon)
    return (widened * factor).astype(jnp.bfloat16)


def swiglu_apply(inputs, weights):
    gate = jnp.einsum("thd,hrd->htr", inputs, weights[:, 0], preferred_element_type=jnp.float32)
    upward = jnp.einsum("thd,hrd->htr", inputs, weights[:, 1], preferred_element_type=jnp.float32)
    hidden = (jax.nn.silu(gate) * upward).astype(jnp.bfloat16)
    return jnp.einsum("htr,hrd->htd", hidden, weights[:, 2], preferred_element_type=jnp.float32)


def window_attention(query_own, key_own, value_own, key_prior, value_prior, first_block):
    tok_rows = query_own.shape[0]
    per_rep = query_own.shape[1]
    width = query_own.shape[2]
    block_rows = min(tok_rows, 512)
    block_count = tok_rows // block_rows
    key_window = jnp.concatenate([key_prior, key_own], axis=0)
    value_window = jnp.concatenate([value_prior, value_own], axis=0)
    score_scale = width ** (-0.5)
    position = jnp.arange(2 * tok_rows)
    valid = jnp.logical_or(position >= tok_rows, jnp.logical_not(first_block))
    query_blocks = query_own.reshape(block_count, block_rows, per_rep, width)

    def one_block(query_block):
        scores = (
            jnp.einsum("tad,sad->ats", query_block, key_window, preferred_element_type=jnp.float32)
            * score_scale
        )
        scores = jnp.where(valid[None, None, :], scores, -jnp.inf)
        peak = jnp.max(scores, axis=-1, keepdims=True)
        weights = jnp.exp(scores - peak)
        probs = (weights / jnp.sum(weights, axis=-1, keepdims=True)).astype(jnp.bfloat16)
        return jnp.einsum("ats,sad->tad", probs, value_window, preferred_element_type=jnp.float32)

    return lax.map(one_block, query_blocks).reshape(tok_rows, per_rep, width)


def on_device(queries, key_vectors, values, learn_rates, fast_weights, momentum):
    tok_rows = queries.shape[0]
    head_count = fast_weights.shape[0]
    width = fast_weights.shape[3]
    rep_count = lax.axis_size("rep")
    per_rep = head_count // rep_count
    rep_index = lax.axis_index("rep")
    ctx_index = lax.axis_index("ctx")
    total_tokens = tok_rows * lax.axis_size("ctx")
    query_heads = queries.reshape(tok_rows, head_count, width)
    key_heads = key_vectors.reshape(tok_rows, head_count, width)
    value_heads = values.reshape(tok_rows, head_count, width)
    query_unit = unit_rows(query_heads)
    key_unit = unit_rows(key_heads)
    token_scale = float(total_tokens) ** (-0.5)
    cotangent = (
        -(learn_rates.T[:, :, None] * token_scale) * value_heads.astype(jnp.float32)
    ).astype(jnp.bfloat16)
    weight_rows = lax.all_gather(fast_weights.astype(jnp.bfloat16), "ctx", axis=2, tiled=True)
    gate = jnp.einsum(
        "thd,hrd->htr", key_unit, weight_rows[:, 0], preferred_element_type=jnp.float32
    )
    upward = jnp.einsum(
        "thd,hrd->htr", key_unit, weight_rows[:, 1], preferred_element_type=jnp.float32
    )
    back = jnp.einsum(
        "thd,hrd->htr", cotangent, weight_rows[:, 2], preferred_element_type=jnp.float32
    )
    sigma = jax.nn.sigmoid(gate)
    activated = jax.nn.silu(gate)
    hidden = (activated * upward).astype(jnp.bfloat16)
    gate_back = (back * upward * sigma * (1.0 + gate * (1.0 - sigma))).astype(jnp.bfloat16)
    up_back = (back * activated).astype(jnp.bfloat16)
    grad_gate = jnp.einsum("htr,thd->hrd", gate_back, key_unit, preferred_element_type=jnp.float32)
    grad_up = jnp.einsum("htr,thd->hrd", up_back, key_unit, preferred_element_type=jnp.float32)
    grad_down = jnp.einsum("htr,thd->hrd", hidden, cotangent, preferred_element_type=jnp.float32)
    gradient = jnp.stack([grad_gate, grad_up, grad_down], axis=1)
    share = lax.psum_scatter(
        gradient.astype(jnp.bfloat16), "ctx", scatter_dimension=2, tiled=True
    ).astype(jnp.float32)
    fast_updated = fast_weights - (momentum_decay * momentum + share)
    new_rows = lax.all_gather(fast_updated.astype(jnp.bfloat16), "ctx", axis=2, tiled=True)
    own_start = rep_index * per_rep
    partial_out = swiglu_apply(query_unit, new_rows)
    traded = lax.all_to_all(
        partial_out.astype(jnp.bfloat16), "rep", split_axis=0, concat_axis=0, tiled=True
    ).astype(partial_out.dtype)
    fast_out = jnp.sum(traded.reshape(rep_count, per_rep, tok_rows, width), axis=0)
    attend_query = lax.dynamic_slice_in_dim(query_heads, own_start, per_rep, 1)
    attend_key = lax.dynamic_slice_in_dim(key_heads, own_start, per_rep, 1)
    attend_value = lax.dynamic_slice_in_dim(value_heads, own_start, per_rep, 1)
    key_prior, value_prior = passed_along((attend_key, attend_value), "ctx", 1)
    attended = window_attention(
        attend_query, attend_key, attend_value, key_prior, value_prior, ctx_index == 0
    )
    combined = attended + jnp.transpose(fast_out, (1, 0, 2))
    layer_output = combined.astype(jnp.bfloat16).reshape(tok_rows, per_rep * width)
    return (layer_output, fast_updated)


def solution(mesh):
    return jax.shard_map(
        on_device,
        mesh=mesh,
        in_specs=(
            P(("groups", "ctx"), "head"),
            P(("groups", "ctx"), "head"),
            P(("groups", "ctx"), "head"),
            P("head", ("groups", "ctx")),
            P(("groups", "head"), None, ("ctx", "rep"), None),
            P(("groups", "head"), None, ("ctx", "rep"), None),
        ),
        out_specs=(
            P(("groups", "ctx"), ("head", "rep")),
            P(("groups", "head"), None, ("ctx", "rep"), None),
        ),
        check_vma=False,
    )
```

profile of v0, /device:TPU:0, one launch (start us, length us, event | category | flops | bytes accessed | tf_op | source)
XLA Modules:
  0.0 324.0 jit_solution(14371064781295452740)
XLA Ops:
  7.2 0.0 copy-start.4
  7.2 0.0 all-gather.3.cloned.1.call-start
  7.2 2.9 copy.69
  10.1 0.0 copy-start.5
  10.1 0.0 all-gather.3.cloned.1.call-update
  10.2 0.0 copy-start.6
  10.2 0.0 reduce-scatter.2.cloned.1.call-start
  10.2 0.0 copy-done.4
  10.2 0.3 copy.36
  10.6 0.7 copy-done.5
  11.2 0.3 copy.33
  11.5 0.0 copy-start.2
  11.6 0.1 fusion.15
  11.7 0.0 copy-done.6
  11.7 93.9 %all-gather.3.cloned.1.call-done = bf16[4,3,320,640]{3,2,0,1:T(8,128)(2,1)} async-done(((bf16[4,3,80,640]{3,2,0,1:T(8,128)(2,1)}), bf16[4,3,320,640]{3,2,0,1:T(8,128)(2,1)}) %all-gather.3.cloned.1.call-update) | async-done | bytes 4915216 | tf_op jit(solution)/shard_map/all_gather | solution.py:74
  105.7 2.0 fusion.6
  107.7 2.0 fusion.8
  109.7 0.6 fusion.10
  110.3 2.0 fusion.7
  112.3 0.7 fusion.9
  113.0 0.0 copy-done.2
  113.0 0.6 fusion.11
  113.6 2.8 pad_maximum_fusion
  116.5 0.0 copy-start
  116.5 0.0 reduce-scatter.2.cloned.1.call-update
  116.5 0.0 all-gather.5.cloned.1.call-start
  116.5 87.0 %reduce-scatter.2.cloned.1.call-done = bf16[4,3,80,640]{3,2,0,1:T(8,128)(2,1)} async-done(((bf16[4,3,320,640]{3,2,0,1:T(8,128)(2,1)}), bf16[4,3,80,640]{3,2,0,1:T(8,128)(2,1)}) %reduce-scatter.2.cloned.1.call-update) | async-done | bytes 1228816 | tf_op jit(solution)/shard_map/reduce_scatter | solution.py:93
  203.5 0.0 copy-done
  203.5 4.4 %fusion.88 = (bf16[4,3,80,640]{3,2,0,1:T(8,128)(2,1)}, f32[4,3,80,640]{3,2,0,1:T(8,128)}) fusion(bf16[4,3,80,640]{3,2,0,1:T(8,128)(2,1)} %reduce-scatter.2.cloned.1.call-done, f32[4,3,80,640]{3,2,1,0:T(8,128)} %param.11, f32[4,3,80,640]{3,2,1,0:T(8,128)S(1)} %copy-done), kind=kLoop, calls=%fused_computation.86 | loop fusion | flops 3072000 | bytes 9830400 | tf_op jit(solution)/shard_map/convert_element_type | solution.py:97
  207.9 0.0 copy-start.3
  207.9 0.0 all-gather.5.cloned.1.call-update
  207.9 0.2 copy.61
  208.1 4.1 %collective-permute-start.1 = (bf16[128,2,640]{2,0,1:T(8,128)(2,1)S(1)}, bf16[128,2,640]{2,0,1:T(8,128)(2,1)}, u32[]{:S(2)}, u32[]{:S(2)}) collective-permute-start(bf16[128,2,640]{2,0,1:T(8,128)(2,1)S(1)} %copy.61), channel_id=1, source_target_pairs={{0,4},{4,8},{8,12},{1,5},{5,9},{9,13},{2,6},{6,10},{10,14},{3,7},{... | collective-permute-start | bytes 983048 | tf_op jit(solution)/shard_map/ppermute | solution.py:13
  212.2 0.0 copy-done.3
  212.3 0.7 constant_dynamic-slice_fusion.1
  213.0 0.0 copy-start.1
  213.0 4.1 %collective-permute-start = (bf16[128,2,640]{0,2,1:T(8,128)(2,1)}, bf16[128,2,640]{0,2,1:T(8,128)(2,1)}, u32[]{:S(2)}, u32[]{:S(2)}) collective-permute-start(bf16[128,2,640]{0,2,1:T(8,128)(2,1)} %constant_dynamic-slice_fusion.1), channel_id=1, source_target_pairs={{0,4},{4,8},{8,12},{1,5},{5,9},{9,13},{2,6},{6,10},{10,14},{3,7},{... | collective-permute-start | bytes 983048 | tf_op jit(solution)/shard_map/ppermute | solution.py:13
  217.1 1.4 copy.34
  218.5 0.1 fusion.13
  218.7 2.9 collective-permute-done.1
  221.7 1.5 fusion.90
  223.2 0.0 copy-done.1
  223.2 1.6 copy.51
  224.8 80.2 %all-gather.5.cloned.1.call-done = bf16[4,3,320,640]{3,2,0,1:T(8,128)(2,1)} async-done(((bf16[4,3,80,640]{3,2,0,1:T(8,128)(2,1)}), bf16[4,3,320,640]{3,2,0,1:T(8,128)(2,1)}) %all-gather.5.cloned.1.call-update) | async-done | bytes 4915216 | tf_op jit(solution)/shard_map/all_gather | solution.py:97
  305.0 2.0 fusion.5
  307.0 2.9 fusion.12
  310.0 4.3 %all_to_all.5 = bf16[4,128,640]{2,1,0:T(8,128)(2,1)S(1)} all-to-all(bf16[4,128,640]{2,1,0:T(8,128)(2,1)S(1)} %fusion.12), channel_id=1, replica_groups=mesh['groups'=2,'ctx'=4,'head'=2,'rep'=2] {'rep'}, dimensions={0} | all-to-all | bytes 1310720 | tf_op jit(solution)/shard_map/all_to_all | solution.py:100
  314.2 0.1 convert_reduce_fusion
  314.3 0.2 copy.49
  314.5 0.0 collective-permute-done
  314.6 2.0 fusion.20
  316.5 0.9 copy.50
  (5 shorter events, 0.1 us)
Async XLA Ops:
  7.2 3.1 copy-start.4
  7.2 98.5 %all-gather.3.cloned.1.call-start = ((), (), s32[]{:S(2)}) async-start(), calls=%async_computation.2 | async-start | bytes 6144000 | tf_op jit(solution)/shard_map/all_gather | solution.py:74
  10.1 1.1 copy-start.5
  10.2 1.6 copy-start.6
  10.2 193.3 %reduce-scatter.2.cloned.1.call-start = ((), (), s32[]{:S(2)}) async-start(), calls=%async_computation.3 | async-start | bytes 6144000 | tf_op jit(solution)/shard_map/reduce_scatter | solution.py:93
  11.5 101.5 %copy-start.2 = (bf16[128,2560]{0,1:T(8,128)(2,1)}, bf16[128,2560]{0,1:T(8,128)(2,1)S(1)}, u32[]{:S(2)}) copy-start(bf16[128,2560]{0,1:T(8,128)(2,1)S(1)} %copy.33) | copy-start | bytes 1966084
  116.5 87.0 %copy-start = (f32[4,3,80,640]{3,2,1,0:T(8,128)S(1)}, f32[4,3,80,640]{3,2,1,0:T(8,128)}, u32[]{:S(2)}) copy-start(f32[4,3,80,640]{3,2,1,0:T(8,128)} %param.10) | copy-start | bytes 7372804
  116.5 188.5 %all-gather.5.cloned.1.call-start = ((), (), s32[]{:S(2)}) async-start(), calls=%async_computation.4 | async-start | bytes 6144000 | tf_op jit(solution)/shard_map/all_gather | solution.py:97
  207.9 4.4 %copy-start.3 = (bf16[128,2560]{0,1:T(8,128)(2,1)S(1)}, bf16[128,2560]{0,1:T(8,128)(2,1)}, u32[]{:S(2)}) copy-start(bf16[128,2560]{0,1:T(8,128)(2,1)} %copy-done.2) | copy-start | bytes 1966084
  208.1 13.5 %collective-permute-start.1 = (bf16[128,2,640]{2,0,1:T(8,128)(2,1)S(1)}, bf16[128,2,640]{2,0,1:T(8,128)(2,1)}, u32[]{:S(2)}, u32[]{:S(2)}) collective-permute-start(bf16[128,2,640]{2,0,1:T(8,128)(2,1)S(1)} %copy.61), channel_id=1, source_target_pairs={{0,4},{4,8},{8,12},{1,5},{5,9},{9,13},{2,6},{6,10},{10,14},{3,7},{... | collective-permute-start | bytes 983048 | tf_op jit(solution)/shard_map/ppermute | solution.py:13
  213.0 10.2 %copy-start.1 = (f32[4,3,80,640]{3,2,0,1:T(8,128)S(1)}, f32[4,3,80,640]{3,2,0,1:T(8,128)}, u32[]{:S(2)}) copy-start(f32[4,3,80,640]{3,2,0,1:T(8,128)} %get-tuple-element.27) | copy-start | bytes 7372804
  213.0 101.5 %collective-permute-start = (bf16[128,2,640]{0,2,1:T(8,128)(2,1)}, bf16[128,2,640]{0,2,1:T(8,128)(2,1)}, u32[]{:S(2)}, u32[]{:S(2)}) collective-permute-start(bf16[128,2,640]{0,2,1:T(8,128)(2,1)} %constant_dynamic-slice_fusion.1), channel_id=1, source_target_pairs={{0,4},{4,8},{8,12},{1,5},{5,9},{9,13},{2,6},{6,10},{10,14},{3,7},{... | collective-permute-start | bytes 983048 | tf_op jit(solution)/shard_map/ppermute | solution.py:13
Sparse Core Ops, SparseCore 0:
  10.3 95.3 all-gather.2
  116.6 86.8 reduce-scatter.1
  208.0 96.9 all-gather.4
where the time goes:
time: 325 us; the launch traced here: 324 us
  waiting for transfers between devices  264 us (81%)
  matrix products  16.3 us (5%)
  between operations  13.9 us (4%)
  local copies, waits for them, and re-layouts  9.4 us (3%)
  starting transfers between devices  8.31 us (3%)
  other arithmetic  7.58 us (2%)
  blocking collectives  4.26 us (1%)
    all_gather x1, waiting for transfers between devices, on_device(): lax.all_gather(fast_weights.astype(jnp.bfloat16), 'ctx', axis=2, tiled=True)  93.9 us
    reduce_scatter x1, waiting for transfers between devices, on_device(): lax.psum_scatter(gradient.astype(jnp.bfloat16), 'ctx', scatter_dimension=...  87 us
    all_gather x1, waiting for transfers between devices, on_device(): lax.all_gather(fast_updated.astype(jnp.bfloat16), 'ctx', axis=2, tiled=True)  80.2 us
    unnamed x21, local copies, waits for them, and re-layouts  8.4 us
    ppermute x2, starting transfers between devices, passed_along(): lax.ppermute(value, axis, [(source, source + steps) for source in range(i...  8.19 us
  transfers between devices with their start and end apart: 5, of which 4 were waited for; matrix products, arithmetic and copies ran while one was open for 4% of the time, Pallas kernels for 0%

commit v1 on v0

--- a/solution.py
+++ b/solution.py
@@ -1,16 +1,26 @@
+import functools
+
 import jax
 import jax.numpy as jnp
 from jax import lax
+from jax.experimental import pallas as pl
+from jax.experimental.pallas import tpu as pltpu
 from jax.sharding import PartitionSpec as P
 
 epsilon = 1e-06
 momentum_decay = 0.9
+NT = (((1,), (1,)), ((), ()))
 
 
 def passed_along(value, axis, steps):
     count = lax.axis_size(axis)
     initial, last = (max(0, -steps), min(count, count - steps))
     return lax.ppermute(value, axis, [(source, source + steps) for source in range(initial, last)])
+
+
+def ring(value, axis, steps=1):
+    count = lax.axis_size(axis)
+    return lax.ppermute(value, axis, [(source, (source + steps) % count) for source in range(count)])
 
 
 def unit_rows(tensor):
@@ -53,7 +63,7 @@
     return lax.map(one_block, query_blocks).reshape(tok_rows, per_rep, width)
 
 
-def on_device(queries, key_vectors, values, learn_rates, fast_weights, momentum):
+def weights_travel(queries, key_vectors, values, learn_rates, fast_weights, momentum):
     tok_rows = queries.shape[0]
     head_count = fast_weights.shape[0]
     width = fast_weights.shape[3]
@@ -113,6 +123,204 @@
     return (layer_output, fast_updated)
 
 
+def gradient_body(slots, token_scale, *refs):
+    keys, vals, rates = refs[:slots], refs[slots : 2 * slots], refs[2 * slots : 3 * slots]
+    low_own, low_par, base_own, base_par, new_own, new_par, new_low, unit, value, low = refs[3 * slots :]
+    rows = keys[0].shape[0]
+    hid = low_own.shape[2]
+    for s in range(slots):
+        here = pl.ds(s * rows, rows)
+        unit[here, :] = unit_rows(keys[s][...])
+        value[here, :] = vals[s][...]
+    for m in range(3):
+        low[pl.ds(2 * m * hid, hid), :] = low_own[0, m]
+        low[pl.ds((2 * m + 1) * hid, hid), :] = low_par[0, m]
+    rate = -(jnp.concatenate([r[0] for r in rates], axis=-1) * token_scale)
+    fed = lax.dot_general(low[: 4 * hid, :], unit[...], NT, preferred_element_type=jnp.float32)
+    gate, upward = fed[: 2 * hid], fed[2 * hid :]
+    back = lax.dot_general(low[4 * hid :, :], value[...], NT, preferred_element_type=jnp.float32) * rate
+    sigma = jax.nn.sigmoid(gate)
+    activated = gate * sigma
+    hidden = (activated * upward * rate).astype(jnp.bfloat16)
+    gate_back = (back * upward * sigma * (1.0 + gate * (1.0 - sigma))).astype(jnp.bfloat16)
+    up_back = (back * activated).astype(jnp.bfloat16)
+    for m, (left, right) in enumerate(((gate_back, unit), (up_back, unit), (hidden, value))):
+        grad = jnp.dot(left, right[...], preferred_element_type=jnp.float32)
+        fresh_own = base_own[0, m] - grad[:hid]
+        fresh_par = base_par[0, m] - grad[hid:]
+        new_own[0, m] = fresh_own
+        new_par[0, m] = fresh_par
+        new_low[0, pl.ds(2 * m * hid, hid), :] = fresh_own.astype(jnp.bfloat16)
+        new_low[0, pl.ds((2 * m + 1) * hid, hid), :] = fresh_par.astype(jnp.bfloat16)
+
+
+def gradient_step(keys, vals, rates, low_own, low_par, base_own, base_par):
+    slots = len(keys)
+    rows = keys[0].shape[0]
+    heads, _, hid, width = low_own.shape
+    token_scale = float(slots * rows) ** (-0.5)
+    token_spec = pl.BlockSpec((rows, width), lambda h: (0, h))
+    rate_spec = pl.BlockSpec((1, 1, rows), lambda h: (h, 0, 0))
+    weight_spec = pl.BlockSpec((1, 3, hid, width), lambda h: (h, 0, 0, 0))
+    low_spec = pl.BlockSpec((1, 6 * hid, width), lambda h: (h, 0, 0))
+    whole = jax.ShapeDtypeStruct(low_own.shape, jnp.float32)
+    work = heads * slots * rows * hid * width
+    return pl.pallas_call(
+        functools.partial(gradient_body, slots, token_scale),
+        out_shape=(whole, whole, jax.ShapeDtypeStruct((heads, 6 * hid, width), jnp.bfloat16)),
+        grid=(heads,),
+        in_specs=[token_spec] * (2 * slots) + [rate_spec] * slots + [weight_spec] * 4,
+        out_specs=(weight_spec, weight_spec, low_spec),
+        scratch_shapes=[
+            pltpu.VMEM((slots * rows, width), jnp.bfloat16),
+            pltpu.VMEM((slots * rows, width), jnp.bfloat16),
+            pltpu.VMEM((6 * hid, width), jnp.bfloat16),
+        ],
+        cost_estimate=pl.CostEstimate(
+            flops=24 * work, bytes_accessed=36 * heads * hid * width, transcendentals=0
+        ),
+        name="gradient_step",
+    )(*keys, *vals, *rates, low_own, low_par, base_own, base_par)
+
+
+def apply_body(query, low, *refs):
+    out = refs[-1]
+    width = low.shape[2]
+    hid = low.shape[1] // 6
+    for h in range(low.shape[0]):
+        columns = slice(h * width, (h + 1) * width)
+        unit = unit_rows(query[:, columns])
+        gate = lax.dot_general(unit, low[h, : 2 * hid, :], NT, preferred_element_type=jnp.float32)
+        upward = lax.dot_general(
+            unit, low[h, 2 * hid : 4 * hid, :], NT, preferred_element_type=jnp.float32
+        )
+        hidden = (gate * jax.nn.sigmoid(gate) * upward).astype(jnp.bfloat16)
+        made = jnp.dot(hidden, low[h, 4 * hid :, :], preferred_element_type=jnp.float32)
+        if len(refs) > 1:
+            made = made + refs[0][:, columns]
+        out[:, columns] = made.astype(out.dtype)
+
+
+def apply_step(query, low, dtype, *more):
+    heads, total, width = low.shape
+    return pl.pallas_call(
+        apply_body,
+        out_shape=jax.ShapeDtypeStruct(query.shape, dtype),
+        cost_estimate=pl.CostEstimate(
+            flops=2 * query.shape[0] * heads * total * width,
+            bytes_accessed=2 * heads * total * width,
+            transcendentals=0,
+        ),
+        name="apply_step",
+    )(query, low, *more)
+
+
+def attend_body(width, first, query, key_own, key_prior, value_own, value_prior, out):
+    rows = query.shape[0]
+    heads = query.shape[1] // width
+    allowed = jnp.where(first[0] != 0, -jnp.inf, 0.0).astype(jnp.float32)
+    for h in range(heads):
+        columns = slice(h * width, (h + 1) * width)
+        part = query[:, columns]
+        near = lax.dot_general(part, key_own[:, columns], NT, preferred_element_type=jnp.float32)
+        far = lax.dot_general(part, key_prior[:, columns], NT, preferred_element_type=jnp.float32)
+        near = near * width ** (-0.5)
+        far = far * width ** (-0.5) + allowed
+        peak = jnp.maximum(
+            jnp.max(near, axis=-1, keepdims=True), jnp.max(far, axis=-1, keepdims=True)
+        )
+        near = jnp.exp(near - peak)
+        far = jnp.exp(far - peak)
+        total = jnp.sum(near, axis=-1, keepdims=True) + jnp.sum(far, axis=-1, keepdims=True)
+        near = (near / total).astype(jnp.bfloat16)
+        far = (far / total).astype(jnp.bfloat16)
+        out[:, columns] = jnp.dot(
+            near, value_own[:, columns], preferred_element_type=jnp.float32
+        ) + jnp.dot(far, value_prior[:, columns], preferred_element_type=jnp.float32)
+
+
+def attend_step(width, first, query, key_own, key_prior, value_own, value_prior):
+    in_vmem = pl.BlockSpec(memory_space=pltpu.VMEM)
+    rows, columns = query.shape
+    return pl.pallas_call(
+        functools.partial(attend_body, width),
+        out_shape=jax.ShapeDtypeStruct(query.shape, jnp.float32),
+        in_specs=[pl.BlockSpec(memory_space=pltpu.SMEM)] + [in_vmem] * 5,
+        out_specs=in_vmem,
+        cost_estimate=pl.CostEstimate(
+            flops=8 * rows * rows * columns, bytes_accessed=14 * rows * columns, transcendentals=0
+        ),
+        name="attend_step",
+    )(first, query, key_own, key_prior, value_own, value_prior)
+
+
+def tokens_travel(queries, key_vectors, values, learn_rates, fast_weights, momentum):
+    head_count = fast_weights.shape[0]
+    width = fast_weights.shape[3]
+    slots = lax.axis_size("ctx")
+    per_rep = head_count // 2
+    rep_index = lax.axis_index("rep")
+    start = rep_index * per_rep
+    away = per_rep - start
+
+    def own_columns(tensor):
+        return lax.dynamic_slice_in_dim(tensor, start * width, per_rep * width, 1)
+
+    def own(tensor):
+        return lax.dynamic_slice_in_dim(tensor, start, per_rep, 0)
+
+    def other(tensor):
+        return lax.dynamic_slice_in_dim(tensor, away, per_rep, 0)
+
+    keys, vals, asked = [own_columns(key_vectors)], [own_columns(values)], [own_columns(queries)]
+    rates = [own(learn_rates)[:, None, :]]
+    for step in range(1, slots):
+        keys.append(ring(keys[-1], "ctx"))
+        vals.append(ring(vals[-1], "ctx"))
+        rates.append(ring(rates[0], "ctx", step))
+    base = fast_weights - momentum_decay * momentum
+    low = fast_weights.astype(jnp.bfloat16)
+    low_par = ring(other(low), "rep")
+    base_par = ring(other(base), "rep")
+    for step in range(1, slots):
+        asked.append(ring(asked[-1], "ctx"))
+    first = (lax.axis_index("ctx") == 0).astype(jnp.int32).reshape(1)
+    attended = attend_step(width, first, asked[0], keys[0], keys[1], vals[0], vals[1])
+    new_own, new_par, new_low = gradient_step(
+        keys, vals, rates, own(low), low_par, own(base), base_par
+    )
+    moving = None
+    for step in range(1, slots):
+        if moving is None:
+            made = apply_step(asked[step], new_low, jnp.bfloat16)
+        else:
+            made = apply_step(asked[step], new_low, jnp.float32)
+            made = (made + moving.astype(jnp.float32)).astype(jnp.bfloat16)
+        moving = ring(made, "ctx")
+    kept = apply_step(asked[0], new_low, jnp.float32, attended)
+    layer_output = (kept + moving.astype(jnp.float32)).astype(jnp.bfloat16)
+    returned = ring(new_par, "rep")
+    fast_updated = jnp.where(
+        rep_index == 0,
+        jnp.concatenate([new_own, returned], axis=0),
+        jnp.concatenate([returned, new_own], axis=0),
+    )
+    return (layer_output, fast_updated)
+
+
+def on_device(queries, key_vectors, values, learn_rates, fast_weights, momentum):
+    slots = lax.axis_size("ctx")
+    fits = (
+        lax.axis_size("rep") == 2
+        and 2 <= slots <= 8
+        and fast_weights.shape[0] % 2 == 0
+        and fast_weights.shape[2] % 16 == 0
+        and queries.shape[0] == 128
+    )
+    program = tokens_travel if fits else weights_travel
+    return program(queries, key_vectors, values, learn_rates, fast_weights, momentum)
+
+
 def solution(mesh):
     return jax.shard_map(
         on_device,

time: 325 us -> 120 us (0.37)
  waiting for transfers between devices: 264 us -> 67.7 us
  Pallas kernels: 0 us -> 21.7 us
  matrix products: 16.3 us -> 0 us
  between operations: 13.9 us -> 0.87 us
  starting transfers between devices: 8.31 us -> 13.9 us
  blocking collectives: 4.26 us -> 0 us
    all_gather x2 -> x0, waiting for transfers between devices: 174 us -> none  [the longest x1 93.9 us: on_device(): lax.all_gather(fast_weights.astype(jnp.bfloat16), 'ctx', axis=2, tiled=True)]
    reduce_scatter x1 -> x0, waiting for transfers between devices: 87 us -> none  [on_device(): lax.psum_scatter(gradient.astype(jnp.bfloat16), 'ctx', scatter_dimension=...]
    ppermute x2 -> x18, waiting for transfers between devices: 2.94 us -> 67.7 us  [ring(): lax.ppermute(value, axis, [(source, (source + steps) % count) for source...]
    pallas_call x0 -> x6, Pallas kernels: none -> 21.7 us  [the longest x4 12.5 us: apply_step(): pl.pallas_call(apply_body, out_shape=jax.ShapeDtypeStruct(query.shape, dt...]
    dot_general x9 -> x0, matrix products: 14.8 us -> none  [the longest x1 2.91 us: swiglu_apply(): jnp.einsum('htr,hrd->htd', hidden, weights[:, 2], preferred_element_type=...]
    unnamed x21 -> x38, local copies, waits for them, and re-layouts: 8.4 us -> 1.54 us
    ppermute x2 -> x18, starting transfers between devices: 8.19 us -> 13.9 us  [ring(): lax.ppermute(value, axis, [(source, (source + steps) % count) for source...]
    all_to_all x1 -> x0, blocking collectives: 4.26 us -> none  [on_device(): lax.all_to_all(partial_out.astype(jnp.bfloat16), 'rep', split_axis=0, con...]
  transfers between devices with their start and end apart: 5 -> 18, of which waited for: 4 -> 12; matrix products, arithmetic and copies ran while one was open for 4% -> 6% of each run, Pallas kernels for 0% -> 18%
where the time goes in v1:
time: 120 us
  waiting for transfers between devices  67.7 us (56%)
  Pallas kernels  21.7 us (18%)
  starting transfers between devices  13.9 us (12%)
  other arithmetic  9.47 us (8%)
  local copies, waits for them, and re-layouts  6.17 us (5%)
    ppermute x18, waiting for transfers between devices, ring(): lax.ppermute(value, axis, [(source, (source + steps) % count) for source...  67.7 us
    ppermute x18, starting transfers between devices, ring(): lax.ppermute(value, axis, [(source, (source + steps) % count) for source...  13.9 us
    pallas_call x4, Pallas kernels, apply_step(): pl.pallas_call(apply_body, out_shape=jax.ShapeDtypeStruct(query.shape, dt...  12.5 us
    pallas_call x1, Pallas kernels, gradient_step(): pl.pallas_call(functools.partial(gradient_body, slots, token_scale), out_...  5.82 us
    sub x1, other arithmetic, tokens_travel(): base = fast_weights - momentum_decay * momentum  3.63 us
    pallas_call x1, Pallas kernels, attend_step(): pl.pallas_call(functools.partial(attend_body, width), out_shape=jax.Shape...  3.37 us
    dynamic_slice x2, local copies, waits for them, and re-layouts, other(): return lax.dynamic_slice_in_dim(tensor, away, per_rep, 0)  2.6 us
  transfers between devices with their start and end apart: 18, of which 12 were waited for; matrix products, arithmetic and copies ran while one was open for 6% of the time, Pallas kernels for 18%

profile of v1, /device:TPU:0, one launch (start us, length us, event | category | flops | bytes accessed | tf_op | source)
XLA Modules:
  0.0 119.8 jit_solution(11769273505909666810)
XLA Ops:
  0.6 0.0 copy-start
  0.7 3.6 %multiply_subtract_fusion = (f32[4,3,80,640]{3,2,1,0:T(8,128)S(1)}, bf16[4,3,80,640]{3,2,1,0:T(8,128)(2,1)S(1)}) fusion(f32[4,3,80,640]{3,2,1,0:T(8,128)} %param.10, f32[4,3,80,640]{3,2,1,0:T(8,128)} %param.11), kind=kLoop, calls=%fused_computation.1 | loop fusion | flops 1843200 | bytes 8601600 | tf_op jit(solution)/shard_map/sub | solution.py:281
  4.3 1.6 %constant_dynamic-slice_fusion = (f32[2,3,80,640]{3,2,1,0:T(8,128)}, f32[2,3,80,640]{3,2,1,0:T(8,128)}) fusion(f32[4,3,80,640]{3,2,1,0:T(8,128)S(1)} %get-tuple-element.10, s32[]{:T(128)S(6)} %select_n.24, s32[]{:T(128)S(6)} %select_n.23), kind=kLoop, calls=%fused_computation.5 | loop fusion | bytes 4915208 | tf_op jit(solution)/shard_map/dynamic_slice | solution.py:273
  5.9 0.5 collective-permute-start.10
  6.4 0.0 copy-done
  6.4 0.0 copy-start.1
  6.4 2.6 %collective-permute-start = (bf16[128,1280]{1,0:T(8,128)(2,1)S(1)}, bf16[128,1280]{1,0:T(8,128)(2,1)S(1)}, u32[]{:S(2)}, u32[]{:S(2)}) collective-permute-start(bf16[128,1280]{1,0:T(8,128)(2,1)S(1)} %constant_dynamic-slice_fusion.6.refs_0_.key_own), channel_id=1, source_target_pairs={{0,4},{4,8},{8,12},{12,0},{1,5},{5,9},{9,13},{13,1},{2,6},{6,10},{... | collective-permute-start | bytes 983048 | tf_op jit(solution)/shard_map/ppermute | solution.py:23
  9.1 1.0 constant_dynamic-slice_fusion.5.refs_4_.value_own
  10.1 0.0 copy-start.2
  10.1 1.6 %collective-permute-start.3 = (bf16[128,1280]{1,0:T(8,128)(2,1)S(1)}, bf16[128,1280]{1,0:T(8,128)(2,1)S(1)}, u32[]{:S(2)}, u32[]{:S(2)}) collective-permute-start(bf16[128,1280]{1,0:T(8,128)(2,1)S(1)} %constant_dynamic-slice_fusion.5.refs_4_.value_own), channel_id=1, source_target_pairs={{0,4},{4,8},{8,12},{12,0},{1,5},{5,9},{9,13},{13,1},{2,6},{6,10},{... | collective-permute-start | bytes 983048 | tf_op jit(solution)/shard_map/ppermute | solution.py:23
  11.7 1.0 constant_dynamic-slice_fusion.2
  12.7 0.0 collective-permute-start.9
  12.7 7.0 %collective-permute-done.refs_1_.key_prior = bf16[128,1280]{1,0:T(8,128)(2,1)S(1)} collective-permute-done((bf16[128,1280]{1,0:T(8,128)(2,1)S(1)}, bf16[128,1280]{1,0:T(8,128)(2,1)S(1)}, u32[]{:S(2)}, u32[]{:S(2)}) %collective-permute-start) | collective-permute-done | bytes 327712 | tf_op jit(solution)/shard_map/ppermute | solution.py:23
  19.7 0.0 collective-permute-start.1
  19.7 7.0 %collective-permute-done.3.refs_5_.value_prior = bf16[128,1280]{1,0:T(8,128)(2,1)S(1)} collective-permute-done((bf16[128,1280]{1,0:T(8,128)(2,1)S(1)}, bf16[128,1280]{1,0:T(8,128)(2,1)S(1)}, u32[]{:S(2)}, u32[]{:S(2)}) %collective-permute-start.3) | collective-permute-done | bytes 327712 | tf_op jit(solution)/shard_map/ppermute | solution.py:23
  26.7 0.0 collective-permute-start.4
  26.7 0.0 copy-done.18
  26.7 0.0 copy-start.14
  26.7 1.6 %collective-permute-start.6 = (f32[2,1,128]{2,1,0:T(1,128)S(1)}, f32[2,1,128]{2,1,0:T(1,128)S(1)}, u32[]{:S(2)}, u32[]{:S(2)}) collective-permute-start(f32[2,1,128]{2,1,0:T(1,128)S(1)} %bitcast.2), channel_id=1, source_target_pairs={{0,4},{4,8},{8,12},{12,0},{1,5},{5,9},{9,13},{13,1},{2,6},{6,10},{... | collective-permute-start | bytes 3080 | tf_op jit(solution)/shard_map/ppermute | solution.py:23
  28.3 12.3 %collective-permute-done.6.refs_9_ = f32[2,1,128]{2,1,0:T(1,128)S(1)} collective-permute-done((f32[2,1,128]{2,1,0:T(1,128)S(1)}, f32[2,1,128]{2,1,0:T(1,128)S(1)}, u32[]{:S(2)}, u32[]{:S(2)}) %collective-permute-start.6) | collective-permute-done | bytes 1056 | tf_op jit(solution)/shard_map/ppermute | solution.py:23
  40.6 0.7 collective-permute-start.7
  41.3 3.7 %collective-permute-done.7.refs_10_ = f32[2,1,128]{2,1,0:T(1,128)S(1)} collective-permute-done((f32[2,1,128]{2,1,0:T(1,128)S(1)}, f32[2,1,128]{2,1,0:T(1,128)S(1)}, u32[]{:S(2)}, u32[]{:S(2)}) %collective-permute-start.7) | collective-permute-done | bytes 1056 | tf_op jit(solution)/shard_map/ppermute | solution.py:23
  45.1 1.7 %collective-permute-start.8 = (f32[2,1,128]{2,1,0:T(1,128)S(1)}, f32[2,1,128]{2,1,0:T(1,128)S(1)}, u32[]{:S(2)}, u32[]{:S(2)}) collective-permute-start(f32[2,1,128]{2,1,0:T(1,128)S(1)} %bitcast.4), channel_id=1, source_target_pairs={{0,12},{4,0},{8,4},{12,8},{1,13},{5,1},{9,5},{13,9},{2,14},{6,2},{... | collective-permute-start | bytes 3080 | tf_op jit(solution)/shard_map/ppermute | solution.py:23
  46.8 1.0 constant_dynamic-slice_fusion.7.query
  47.8 0.0 copy-start.3
  47.8 0.8 collective-permute-done.8.refs_11_
  48.7 0.0 collective-permute-start.11
  48.7 0.0 collective-permute-done.1.refs_2_
  48.7 1.3 %collective-permute-start.2 = (bf16[128,1280]{1,0:T(8,128)(2,1)S(1)}, bf16[128,1280]{1,0:T(8,128)(2,1)S(1)}, u32[]{:S(2)}, u32[]{:S(2)}) collective-permute-start(bf16[128,1280]{1,0:T(8,128)(2,1)S(1)} %collective-permute-done.1.refs_2_), channel_id=1, source_target_pairs={{0,4},{4,8},{8,12},{12,0},{1,5},{5,9},{9,13},{13,1},{2,6},{6,10},{... | collective-permute-start | bytes 983048 | tf_op jit(solution)/shard_map/ppermute | solution.py:23
  50.0 0.0 collective-permute-done.4.refs_6_
  50.0 3.4 %collective-permute-start.5 = (bf16[128,1280]{1,0:T(8,128)(2,1)S(1)}, bf16[128,1280]{1,0:T(8,128)(2,1)S(1)}, u32[]{:S(2)}, u32[]{:S(2)}) collective-permute-start(bf16[128,1280]{1,0:T(8,128)(2,1)S(1)} %collective-permute-done.4.refs_6_), channel_id=1, source_target_pairs={{0,4},{4,8},{8,12},{12,0},{1,5},{5,9},{9,13},{13,1},{2,6},{6,10},{... | collective-permute-start | bytes 983048 | tf_op jit(solution)/shard_map/ppermute | solution.py:23
  53.3 7.7 %collective-permute-done.11.query = bf16[128,1280]{1,0:T(8,128)(2,1)S(1)} collective-permute-done((bf16[128,1280]{1,0:T(8,128)(2,1)S(1)}, bf16[128,1280]{1,0:T(8,128)(2,1)S(1)}, u32[]{:S(2)}, u32[]{:S(2)}) %collective-permute-start.11) | collective-permute-done | bytes 327712 | tf_op jit(solution)/shard_map/ppermute | solution.py:23
  61.0 0.0 collective-permute-start.12
  61.0 0.0 collective-permute-done.9.refs_13_
  61.1 7.0 %collective-permute-done.2.refs_3_ = bf16[128,1280]{1,0:T(8,128)(2,1)S(1)} collective-permute-done((bf16[128,1280]{1,0:T(8,128)(2,1)S(1)}, bf16[128,1280]{1,0:T(8,128)(2,1)S(1)}, u32[]{:S(2)}, u32[]{:S(2)}) %collective-permute-start.2) | collective-permute-done | bytes 327712 | tf_op jit(solution)/shard_map/ppermute | solution.py:23
  68.1 7.0 %collective-permute-done.5.refs_7_ = bf16[128,1280]{1,0:T(8,128)(2,1)S(1)} collective-permute-done((bf16[128,1280]{1,0:T(8,128)(2,1)S(1)}, bf16[128,1280]{1,0:T(8,128)(2,1)S(1)}, u32[]{:S(2)}, u32[]{:S(2)}) %collective-permute-start.5) | collective-permute-done | bytes 327712 | tf_op jit(solution)/shard_map/ppermute | solution.py:23
  75.1 0.0 copy-done.11
  75.1 0.0 collective-permute-done.10.refs_15_
  75.1 0.7 copy-done.12
  75.8 0.0 copy-done.4
  75.9 5.8 %gradient_step.1 = (f32[2,3,80,640]{3,2,1,0:T(8,128)}, f32[2,3,80,640]{3,2,1,0:T(8,128)}, bf16[2,480,640]{2,1,0:T(8,128)(2,1)}) custom-call(bf16[128,1280]{1,0:T(8,128)(2,1)} %copy-done.1, bf16[128,1280]{1,0:T(8,128)(2,1)} %copy-done.4, bf16[128,1280]{1,0:T(8,128)(2,1)} %copy-done.9, bf16[128,1280]{1,0:T(8,128)(2,1)} %copy-done.11, ...), custom_call_target="tpu_custom_call" | custom-call | flops 1258291200 | bytes 3686400 | tf_op jit(solution)/shard_map/gradient_step/pallas_call | solution.py:168
  81.7 0.0 copy-done.3
  81.7 0.0 copy-done.8
  81.7 3.0 %apply_step.7 = bf16[128,1280]{1,0:T(8,128)(2,1)} custom-call(bf16[128,1280]{1,0:T(8,128)(2,1)} %copy-done.8, bf16[2,480,640]{2,1,0:T(8,128)(2,1)} %get-tuple-element.5.low), custom_call_target="tpu_custom_call" | custom-call | flops 157286400 | bytes 1228800 | tf_op jit(solution)/shard_map/apply_step/pallas_call | solution.py:206
  84.7 0.0 collective-permute-start.14
  84.7 0.0 collective-permute-done.12.query
  84.7 0.2 collective-permute-start.13
  85.0 3.1 %apply_step.6 = f32[128,1280]{1,0:T(8,128)} custom-call(bf16[128,1280]{1,0:T(8,128)(2,1)} %collective-permute-done.12.query, bf16[2,480,640]{2,1,0:T(8,128)(2,1)} %get-tuple-element.5.low), custom_call_target="tpu_custom_call" | custom-call | flops 157286400 | bytes 1228800 | tf_op jit(solution)/shard_map/apply_step/pallas_call | solution.py:206
  88.0 8.0 %collective-permute-done.14 = bf16[128,1280]{1,0:T(8,128)(2,1)S(1)} collective-permute-done((bf16[128,1280]{1,0:T(8,128)(2,1)}, bf16[128,1280]{1,0:T(8,128)(2,1)S(1)}, u32[]{:S(2)}, u32[]{:S(2)}) %collective-permute-start.14) | collective-permute-done | bytes 327712 | tf_op jit(solution)/shard_map/ppermute | solution.py:23
  96.0 1.1 add_convert_fusion.2
  97.2 0.1 collective-permute-start.15
  97.2 0.1 collective-permute-start.17
  97.3 3.5 %collective-permute-done.13.query = bf16[128,1280]{1,0:T(8,128)(2,1)S(1)} collective-permute-done((bf16[128,1280]{1,0:T(8,128)(2,1)}, bf16[128,1280]{1,0:T(8,128)(2,1)S(1)}, u32[]{:S(2)}, u32[]{:S(2)}) %collective-permute-start.13) | collective-permute-done | bytes 327712 | tf_op jit(solution)/shard_map/ppermute | solution.py:23
  100.8 0.7 copy-done.13
  101.6 3.1 %apply_step.5 = f32[128,1280]{1,0:T(8,128)} custom-call(bf16[128,1280]{1,0:T(8,128)(2,1)} %copy-done.13, bf16[2,480,640]{2,1,0:T(8,128)(2,1)} %get-tuple-element.5.low), custom_call_target="tpu_custom_call" | custom-call | flops 157286400 | bytes 1228800 | tf_op jit(solution)/shard_map/apply_step/pallas_call | solution.py:206
  104.6 1.5 %collective-permute-done.15 = bf16[128,1280]{1,0:T(8,128)(2,1)S(1)} collective-permute-done((bf16[128,1280]{1,0:T(8,128)(2,1)S(1)}, bf16[128,1280]{1,0:T(8,128)(2,1)S(1)}, u32[]{:S(2)}, u32[]{:S(2)}) %collective-permute-start.15) | collective-permute-done | bytes 327712 | tf_op jit(solution)/shard_map/ppermute | solution.py:23
  106.1 1.1 add_convert_fusion.1
  107.2 0.1 collective-permute-start.16
  107.3 3.4 %attend_step.1.refs_0_ = f32[128,1280]{1,0:T(8,128)} custom-call(s32[1]{0:T(128)} %bitcast.1.first, bf16[128,1280]{1,0:T(8,128)(2,1)} %copy-done.3, bf16[128,1280]{1,0:T(8,128)(2,1)} %copy-done.1, bf16[128,1280]{1,0:T(8,128)(2,1)} %copy-done.4, bf16[128,1280]{1,0:T(8,128)(2,1)} %copy-done.2, bf16[128,1280]{1,0:T(8,128)(2,1)} %copy-done.5), custom_call_target="tpu_custom_call" | custom-call | flops 167772160 | bytes 2293760 | tf_op jit(solution)/shard_map/attend_step/pallas_call | solution.py:245
  110.7 3.3 %apply_step.4 = f32[128,1280]{1,0:T(8,128)} custom-call(bf16[128,1280]{1,0:T(8,128)(2,1)} %copy-done.3, bf16[2,480,640]{2,1,0:T(8,128)(2,1)} %get-tuple-element.5.low, f32[128,1280]{1,0:T(8,128)} %attend_step.1.refs_0_), custom_call_target="tpu_custom_call" | custom-call | flops 157286400 | bytes 1228800 | tf_op jit(solution)/shard_map/apply_step/pallas_call | solution.py:206
  114.0 2.2 %collective-permute-done.16 = bf16[128,1280]{1,0:T(8,128)(2,1)} collective-permute-done((bf16[128,1280]{1,0:T(8,128)(2,1)S(1)}, bf16[128,1280]{1,0:T(8,128)(2,1)}, u32[]{:S(2)}, u32[]{:S(2)}) %collective-permute-start.16) | collective-permute-done | bytes 327712 | tf_op jit(solution)/shard_map/ppermute | solution.py:23
  116.3 1.9 %add_convert_fusion = bf16[128,1280]{1,0:T(8,128)(2,1)} fusion(f32[128,1280]{1,0:T(8,128)} %apply_step.4, bf16[128,1280]{1,0:T(8,128)(2,1)} %collective-permute-done.16), kind=kLoop, calls=%fused_computation.2 | loop fusion | flops 491520 | bytes 1310720 | tf_op jit(solution)/shard_map/convert_element_type | solution.py:301
  118.2 0.0 collective-permute-done.17
  118.2 1.6 %maximum_select_fusion = f32[4,3,80,640]{3,2,1,0:T(8,128)} fusion(f32[2,3,80,640]{3,2,1,0:T(8,128)S(1)} %collective-permute-done.17, f32[2,3,80,640]{3,2,1,0:T(8,128)S(1)} %copy-done.6, pred[]{:T(512)S(6)} %eq.7), kind=kLoop, calls=%fused_computation | loop fusion | flops 1843200 | bytes 4915201 | tf_op jit(solution)/shard_map/jit(_where)/select_n | solution.py:303
  (27 shorter events, 0.1 us)
Async XLA Ops:
  0.6 5.8 %copy-start = (bf16[128,2560]{1,0:T(8,128)(2,1)S(1)}, bf16[128,2560]{1,0:T(8,128)(2,1)}, u32[]{:S(2)}) copy-start(bf16[128,2560]{1,0:T(8,128)(2,1)} %param.7) | copy-start | bytes 1966084
  5.9 20.8 %copy-start.18 = (f32[4,128]{1,0:T(4,128)S(1)}, f32[4,128]{1,0:T(4,128)}, u32[]{:S(2)}) copy-start(f32[4,128]{1,0:T(4,128)} %param.9) | copy-start | bytes 6148
  5.9 69.2 %collective-permute-start.10 = (f32[2,3,80,640]{3,2,1,0:T(8,128)}, f32[2,3,80,640]{3,2,1,0:T(8,128)}, u32[]{:S(2)}, u32[]{:S(2)}) collective-permute-start(f32[2,3,80,640]{3,2,1,0:T(8,128)} %get-tuple-element.8), channel_id=1, source_target_pairs={{0,1},{1,0},{2,3},{3,2},{4,5},{5,4},{6,7},{7,6},{8,9},{9,8},{10,11... | collective-permute-start | bytes 3686408 | tf_op jit(solution)/shard_map/ppermute | solution.py:23
  6.4 69.4 %copy-start.1 = (bf16[128,1280]{1,0:T(8,128)(2,1)}, bf16[128,1280]{1,0:T(8,128)(2,1)S(1)}, u32[]{:S(2)}) copy-start(bf16[128,1280]{1,0:T(8,128)(2,1)S(1)} %constant_dynamic-slice_fusion.6.refs_0_.key_own) | copy-start | bytes 983044
  6.4 13.2 %collective-permute-start = (bf16[128,1280]{1,0:T(8,128)(2,1)S(1)}, bf16[128,1280]{1,0:T(8,128)(2,1)S(1)}, u32[]{:S(2)}, u32[]{:S(2)}) collective-permute-start(bf16[128,1280]{1,0:T(8,128)(2,1)S(1)} %constant_dynamic-slice_fusion.6.refs_0_.key_own), channel_id=1, source_target_pairs={{0,4},{4,8},{8,12},{12,0},{1,5},{5,9},{9,13},{13,1},{2,6},{6,10},{... | collective-permute-start | bytes 983048 | tf_op jit(solution)/shard_map/ppermute | solution.py:23
  10.1 65.8 %copy-start.2 = (bf16[128,1280]{1,0:T(8,128)(2,1)}, bf16[128,1280]{1,0:T(8,128)(2,1)S(1)}, u32[]{:S(2)}) copy-start(bf16[128,1280]{1,0:T(8,128)(2,1)S(1)} %constant_dynamic-slice_fusion.5.refs_4_.value_own) | copy-start | bytes 983044
  10.1 16.6 %collective-permute-start.3 = (bf16[128,1280]{1,0:T(8,128)(2,1)S(1)}, bf16[128,1280]{1,0:T(8,128)(2,1)S(1)}, u32[]{:S(2)}, u32[]{:S(2)}) collective-permute-start(bf16[128,1280]{1,0:T(8,128)(2,1)S(1)} %constant_dynamic-slice_fusion.5.refs_4_.value_own), channel_id=1, source_target_pairs={{0,4},{4,8},{8,12},{12,0},{1,5},{5,9},{9,13},{13,1},{2,6},{6,10},{... | collective-permute-start | bytes 983048 | tf_op jit(solution)/shard_map/ppermute | solution.py:23
  12.7 48.4 %collective-permute-start.9 = (bf16[2,3,80,640]{3,2,1,0:T(8,128)(2,1)S(1)}, bf16[2,3,80,640]{3,2,1,0:T(8,128)(2,1)S(1)}, u32[]{:S(2)}, u32[]{:S(2)}) collective-permute-start(bf16[2,3,80,640]{3,2,1,0:T(8,128)(2,1)S(1)} %get-tuple-element.12), channel_id=1, source_target_pairs={{0,1},{1,0},{2,3},{3,2},{4,5},{5,4},{6,7},{7,6},{8,9},{9,8},{10,11... | collective-permute-start | bytes 1843208 | tf_op jit(solution)/shard_map/ppermute | solution.py:23
  19.7 56.2 %copy-start.4 = (bf16[128,1280]{1,0:T(8,128)(2,1)}, bf16[128,1280]{1,0:T(8,128)(2,1)S(1)}, u32[]{:S(2)}) copy-start(bf16[128,1280]{1,0:T(8,128)(2,1)S(1)} %collective-permute-done.refs_1_.key_prior) | copy-start | bytes 983044
  19.7 29.0 %collective-permute-start.1 = (bf16[128,1280]{1,0:T(8,128)(2,1)S(1)}, bf16[128,1280]{1,0:T(8,128)(2,1)S(1)}, u32[]{:S(2)}, u32[]{:S(2)}) collective-permute-start(bf16[128,1280]{1,0:T(8,128)(2,1)S(1)} %collective-permute-done.refs_1_.key_prior), channel_id=1, source_target_pairs={{0,4},{4,8},{8,12},{12,0},{1,5},{5,9},{9,13},{13,1},{2,6},{6,10},{... | collective-permute-start | bytes 983048 | tf_op jit(solution)/shard_map/ppermute | solution.py:23
  26.7 49.1 %copy-start.5 = (bf16[128,1280]{1,0:T(8,128)(2,1)}, bf16[128,1280]{1,0:T(8,128)(2,1)S(1)}, u32[]{:S(2)}) copy-start(bf16[128,1280]{1,0:T(8,128)(2,1)S(1)} %collective-permute-done.3.refs_5_.value_prior) | copy-start | bytes 983044
  26.7 23.3 %collective-permute-start.4 = (bf16[128,1280]{1,0:T(8,128)(2,1)S(1)}, bf16[128,1280]{1,0:T(8,128)(2,1)S(1)}, u32[]{:S(2)}, u32[]{:S(2)}) collective-permute-start(bf16[128,1280]{1,0:T(8,128)(2,1)S(1)} %collective-permute-done.3.refs_5_.value_prior), channel_id=1, source_target_pairs={{0,4},{4,8},{8,12},{12,0},{1,5},{5,9},{9,13},{13,1},{2,6},{6,10},{... | collective-permute-start | bytes 983048 | tf_op jit(solution)/shard_map/ppermute | solution.py:23
  26.7 49.1 %copy-start.14 = (f32[2,128]{1,0:T(2,128)}, f32[2,128]{1,0:T(2,128)S(1)}, u32[]{:S(2)}) copy-start(f32[2,128]{1,0:T(2,128)S(1)} %constant_dynamic-slice_fusion.4) | copy-start | bytes 3076
  26.7 13.9 %collective-permute-start.6 = (f32[2,1,128]{2,1,0:T(1,128)S(1)}, f32[2,1,128]{2,1,0:T(1,128)S(1)}, u32[]{:S(2)}, u32[]{:S(2)}) collective-permute-start(f32[2,1,128]{2,1,0:T(1,128)S(1)} %bitcast.2), channel_id=1, source_target_pairs={{0,4},{4,8},{8,12},{12,0},{1,5},{5,9},{9,13},{13,1},{2,6},{6,10},{... | collective-permute-start | bytes 3080 | tf_op jit(solution)/shard_map/ppermute | solution.py:23
  40.6 35.2 %copy-start.15 = (f32[2,1,128]{2,1,0:T(1,128)}, f32[2,1,128]{2,1,0:T(1,128)S(1)}, u32[]{:S(2)}) copy-start(f32[2,1,128]{2,1,0:T(1,128)S(1)} %collective-permute-done.6.refs_9_) | copy-start | bytes 3076
  40.6 4.5 %collective-permute-start.7 = (f32[2,1,128]{2,1,0:T(1,128)S(1)}, f32[2,1,128]{2,1,0:T(1,128)S(1)}, u32[]{:S(2)}, u32[]{:S(2)}) collective-permute-start(f32[2,1,128]{2,1,0:T(1,128)S(1)} %bitcast.3), channel_id=1, source_target_pairs={{0,8},{4,12},{8,0},{12,4},{1,9},{5,13},{9,1},{13,5},{2,10},{6,14},... | collective-permute-start | bytes 3080 | tf_op jit(solution)/shard_map/ppermute | solution.py:23
  45.1 30.8 %copy-start.16 = (f32[2,1,128]{2,1,0:T(1,128)}, f32[2,1,128]{2,1,0:T(1,128)S(1)}, u32[]{:S(2)}) copy-start(f32[2,1,128]{2,1,0:T(1,128)S(1)} %collective-permute-done.7.refs_10_) | copy-start | bytes 3076
  45.1 3.6 %collective-permute-start.8 = (f32[2,1,128]{2,1,0:T(1,128)S(1)}, f32[2,1,128]{2,1,0:T(1,128)S(1)}, u32[]{:S(2)}, u32[]{:S(2)}) collective-permute-start(f32[2,1,128]{2,1,0:T(1,128)S(1)} %bitcast.4), channel_id=1, source_target_pairs={{0,12},{4,0},{8,4},{12,8},{1,13},{5,1},{9,5},{13,9},{2,14},{6,2},{... | collective-permute-start | bytes 3080 | tf_op jit(solution)/shard_map/ppermute | solution.py:23
  47.8 33.9 %copy-start.3 = (bf16[128,1280]{1,0:T(8,128)(2,1)}, bf16[128,1280]{1,0:T(8,128)(2,1)S(1)}, u32[]{:S(2)}) copy-start(bf16[128,1280]{1,0:T(8,128)(2,1)S(1)} %constant_dynamic-slice_fusion.7.query) | copy-start | bytes 983044
  48.7 27.2 %copy-start.17 = (f32[2,1,128]{2,1,0:T(1,128)}, f32[2,1,128]{2,1,0:T(1,128)S(1)}, u32[]{:S(2)}) copy-start(f32[2,1,128]{2,1,0:T(1,128)S(1)} %collective-permute-done.8.refs_11_) | copy-start | bytes 3076
  48.7 12.4 %collective-permute-start.11 = (bf16[128,1280]{1,0:T(8,128)(2,1)S(1)}, bf16[128,1280]{1,0:T(8,128)(2,1)S(1)}, u32[]{:S(2)}, u32[]{:S(2)}) collective-permute-start(bf16[128,1280]{1,0:T(8,128)(2,1)S(1)} %constant_dynamic-slice_fusion.7.query), channel_id=1, source_target_pairs={{0,4},{4,8},{8,12},{12,0},{1,5},{5,9},{9,13},{13,1},{2,6},{6,10},{... | collective-permute-start | bytes 983048 | tf_op jit(solution)/shard_map/ppermute | solution.py:23
  48.7 12.4 %copy-start.9 = (bf16[128,1280]{1,0:T(8,128)(2,1)}, bf16[128,1280]{1,0:T(8,128)(2,1)S(1)}, u32[]{:S(2)}) copy-start(bf16[128,1280]{1,0:T(8,128)(2,1)S(1)} %collective-permute-done.1.refs_2_) | copy-start | bytes 983044
  48.7 19.4 %collective-permute-start.2 = (bf16[128,1280]{1,0:T(8,128)(2,1)S(1)}, bf16[128,1280]{1,0:T(8,128)(2,1)S(1)}, u32[]{:S(2)}, u32[]{:S(2)}) collective-permute-start(bf16[128,1280]{1,0:T(8,128)(2,1)S(1)} %collective-permute-done.1.refs_2_), channel_id=1, source_target_pairs={{0,4},{4,8},{8,12},{12,0},{1,5},{5,9},{9,13},{13,1},{2,6},{6,10},{... | collective-permute-start | bytes 983048 | tf_op jit(solution)/shard_map/ppermute | solution.py:23
  50.0 18.1 %copy-start.10 = (bf16[128,1280]{1,0:T(8,128)(2,1)}, bf16[128,1280]{1,0:T(8,128)(2,1)S(1)}, u32[]{:S(2)}) copy-start(bf16[128,1280]{1,0:T(8,128)(2,1)S(1)} %collective-permute-done.4.refs_6_) | copy-start | bytes 983044
  50.0 25.1 %collective-permute-start.5 = (bf16[128,1280]{1,0:T(8,128)(2,1)S(1)}, bf16[128,1280]{1,0:T(8,128)(2,1)S(1)}, u32[]{:S(2)}, u32[]{:S(2)}) collective-permute-start(bf16[128,1280]{1,0:T(8,128)(2,1)S(1)} %collective-permute-done.4.refs_6_), channel_id=1, source_target_pairs={{0,4},{4,8},{8,12},{12,0},{1,5},{5,9},{9,13},{13,1},{2,6},{6,10},{... | collective-permute-start | bytes 983048 | tf_op jit(solution)/shard_map/ppermute | solution.py:23
  61.0 20.7 %copy-start.8 = (bf16[128,1280]{1,0:T(8,128)(2,1)}, bf16[128,1280]{1,0:T(8,128)(2,1)S(1)}, u32[]{:S(2)}) copy-start(bf16[128,1280]{1,0:T(8,128)(2,1)S(1)} %collective-permute-done.11.query) | copy-start | bytes 983044
  61.0 23.7 %collective-permute-start.12 = (bf16[128,1280]{1,0:T(8,128)(2,1)S(1)}, bf16[128,1280]{1,0:T(8,128)(2,1)}, u32[]{:S(2)}, u32[]{:S(2)}) collective-permute-start(bf16[128,1280]{1,0:T(8,128)(2,1)S(1)} %collective-permute-done.11.query), channel_id=1, source_target_pairs={{0,4},{4,8},{8,12},{12,0},{1,5},{5,9},{9,13},{13,1},{2,6},{6,10},{... | collective-permute-start | bytes 983048 | tf_op jit(solution)/shard_map/ppermute | solution.py:23
  61.1 14.8 %copy-start.7 = (bf16[2,3,80,640]{3,2,1,0:T(8,128)(2,1)}, bf16[2,3,80,640]{3,2,1,0:T(8,128)(2,1)S(1)}, u32[]{:S(2)}) copy-start(bf16[2,3,80,640]{3,2,1,0:T(8,128)(2,1)S(1)} %collective-permute-done.9.refs_13_) | copy-start | bytes 1843204
  68.1 7.0 %copy-start.11 = (bf16[128,1280]{1,0:T(8,128)(2,1)}, bf16[128,1280]{1,0:T(8,128)(2,1)S(1)}, u32[]{:S(2)}) copy-start(bf16[128,1280]{1,0:T(8,128)(2,1)S(1)} %collective-permute-done.2.refs_3_) | copy-start | bytes 983044
  75.1 0.7 copy-start.12
  84.7 11.3 %collective-permute-start.14 = (bf16[128,1280]{1,0:T(8,128)(2,1)}, bf16[128,1280]{1,0:T(8,128)(2,1)S(1)}, u32[]{:S(2)}, u32[]{:S(2)}) collective-permute-start(bf16[128,1280]{1,0:T(8,128)(2,1)} %apply_step.7), channel_id=1, source_target_pairs={{0,4},{4,8},{8,12},{12,0},{1,5},{5,9},{9,13},{13,1},{2,6},{6,10},{... | collective-permute-start | bytes 983048 | tf_op jit(solution)/shard_map/ppermute | solution.py:23
  84.7 16.1 %collective-permute-start.13 = (bf16[128,1280]{1,0:T(8,128)(2,1)}, bf16[128,1280]{1,0:T(8,128)(2,1)S(1)}, u32[]{:S(2)}, u32[]{:S(2)}) collective-permute-start(bf16[128,1280]{1,0:T(8,128)(2,1)} %collective-permute-done.12.query), channel_id=1, source_target_pairs={{0,4},{4,8},{8,12},{12,0},{1,5},{5,9},{9,13},{13,1},{2,6},{6,10},{... | collective-permute-start | bytes 983048 | tf_op jit(solution)/shard_map/ppermute | solution.py:23
  97.2 8.9 %collective-permute-start.15 = (bf16[128,1280]{1,0:T(8,128)(2,1)S(1)}, bf16[128,1280]{1,0:T(8,128)(2,1)S(1)}, u32[]{:S(2)}, u32[]{:S(2)}) collective-permute-start(bf16[128,1280]{1,0:T(8,128)(2,1)S(1)} %add_convert_fusion.2), channel_id=1, source_target_pairs={{0,4},{4,8},{8,12},{12,0},{1,5},{5,9},{9,13},{13,1},{2,6},{6,10},{... | collective-permute-start | bytes 983048 | tf_op jit(solution)/shard_map/ppermute | solution.py:23
  97.2 21.0 %collective-permute-start.17 = (f32[2,3,80,640]{3,2,1,0:T(8,128)}, f32[2,3,80,640]{3,2,1,0:T(8,128)S(1)}, u32[]{:S(2)}, u32[]{:S(2)}) collective-permute-start(f32[2,3,80,640]{3,2,1,0:T(8,128)} %get-tuple-element.7), channel_id=1, source_target_pairs={{0,1},{1,0},{2,3},{3,2},{4,5},{5,4},{6,7},{7,6},{8,9},{9,8},{10,11... | collective-permute-start | bytes 3686408 | tf_op jit(solution)/shard_map/ppermute | solution.py:23
  100.8 0.7 copy-start.13
  107.2 9.0 %collective-permute-start.16 = (bf16[128,1280]{1,0:T(8,128)(2,1)S(1)}, bf16[128,1280]{1,0:T(8,128)(2,1)}, u32[]{:S(2)}, u32[]{:S(2)}) collective-permute-start(bf16[128,1280]{1,0:T(8,128)(2,1)S(1)} %add_convert_fusion.1), channel_id=1, source_target_pairs={{0,4},{4,8},{8,12},{12,0},{1,5},{5,9},{9,13},{13,1},{2,6},{6,10},{... | collective-permute-start | bytes 983048 | tf_op jit(solution)/shard_map/ppermute | solution.py:23
  110.7 7.5 %copy-start.6 = (f32[2,3,80,640]{3,2,1,0:T(8,128)S(1)}, f32[2,3,80,640]{3,2,1,0:T(8,128)}, u32[]{:S(2)}) copy-start(f32[2,3,80,640]{3,2,1,0:T(8,128)} %get-tuple-element.6) | copy-start | bytes 3686404
